TPU v7x, 32 devices: a whole 2x2x4 slice. The times are simulated.
32 devices in a mesh: vocab: 4 (over z), rows: 8 (over y, x, core).
Axes of the slice: x: 2, y: 2, z: 4, core: 2. Of those that a mesh axis runs over, the one named last changes fastest.
Arguments:
- trunk_hidden: bfloat16 [32, 7168], P('rows'), may hold values from -8 to 8
- mtp_state: bfloat16 [32, 7168], P('rows'), may hold values from -24 to 24, as said below
- mtp_gain: bfloat16 [7168], replicated, may hold values from 0.099609375 to 1.8984375
- head_weight: bfloat16 [4608, 7168], P(('vocab', 'rows')), may hold values from -0.28347335 to 0.28347335, as said below
- target_ids: int32 [32], replicated, may hold values from 0 to 4607
- mtp_target_ids: int32 [32], replicated, may hold values from 0 to 4607
- attn_values: bfloat16 [32, 16, 128], P('rows'), may hold values from -6 to 6
- out_proj: bfloat16 [2048, 7168], P('rows', 'vocab'), may hold values from -0.125 to 0.125
Outputs:
- grad_trunk: bfloat16 [32, 7168], P('rows')
- grad_residual: bfloat16 [32, 7168], P('rows')
- grad_gain: float32 [7168], replicated
- grad_head: bfloat16 [4608, 7168], P(('vocab', 'rows'))
- grad_attn: bfloat16 [32, 16, 128], P('vocab', 'rows')
- grad_out_proj: bfloat16 [2048, 7168], P('rows', 'vocab')
Inputs may be any that keep to these rules, and one draw needn't show every extreme that they name: `mtp_state`: block outputs; rows differ in scale. `head_weight`: head rows.
All inputs are finite; a program needn't handle non-finite values.
Results may differ from a plain program's by a relative error of at most 0.025.
Values may be sent and summed in bfloat16 or wider, within the bound.
No kernel may reach another device: no remote copies, remote signals or barrier semaphores. Data moves between devices by JAX's collectives and lax.ppermute only.
A program may use at most 64 MiB of HBM per device.

v0:
```python
import jax
import jax.numpy as jnp
from jax import lax
from jax.sharding import PartitionSpec as P

loss_scale = 8.0
mtp_share = 0.3
norm_eps = 1e-06


def merged(shard, axis, combine):
    everything = jax.tree.map(lambda part: lax.all_gather(part, axis), shard)
    initial = jax.tree.map(lambda part: part[0], everything)

    def lap(k, so_far):
        return combine(so_far, jax.tree.map(lambda part: part[k], everything))

    return lax.fori_loop(1, lax.axis_size(axis), lap, initial)


def normalize(state):
    values = state.astype(jnp.float32)
    inverse = lax.rsqrt(jnp.mean(values * values, axis=-1, keepdims=True) + norm_eps)
    return (values * inverse, inverse)


def local(
    trunk_hidden,
    mtp_state,
    mtp_gain,
    head_weight,
    target_ids,
    mtp_target_ids,
    attn_values,
    out_proj,
):
    tok_local = trunk_hidden.shape[0]
    row_count = lax.axis_size("rows")
    vocab_rows = head_weight.shape[0]
    gain = mtp_gain.astype(jnp.float32)
    normed, inverse = normalize(mtp_state)
    mtp_hidden = (normed * gain).astype(jnp.bfloat16)
    stacked = jnp.concatenate([trunk_hidden, mtp_hidden], axis=0)
    targets = jnp.stack(
        [target_ids.reshape(row_count, tok_local), mtp_target_ids.reshape(row_count, tok_local)],
        axis=1,
    ).reshape(-1)
    shares = jnp.stack(
        [
            jnp.full((row_count, tok_local), loss_scale, jnp.float32),
            jnp.full((row_count, tok_local), loss_scale * mtp_share, jnp.float32),
        ],
        axis=1,
    ).reshape(-1)
    block_index = lax.axis_index("vocab") * row_count + lax.axis_index("rows")
    vocab_ids = block_index * vocab_rows + jnp.arange(vocab_rows, dtype=jnp.int32)
    onehot = (targets[:, None] == vocab_ids[None, :]).astype(jnp.float32)
    gathered = lax.all_gather(stacked, "rows", axis=0, tiled=True)
    logits = lax.dot_general(
        gathered, head_weight, (((1,), (1,)), ((), ())), preferred_element_type=jnp.float32
    )
    local_max = jnp.max(logits, axis=1)
    local_total = jnp.sum(jnp.exp(logits - local_max[:, None]), axis=1)

    def combine(first, second):
        upper = jnp.maximum(first[0], second[0])
        return (
            upper,
            first[1] * jnp.exp(first[0] - upper) + second[1] * jnp.exp(second[0] - upper),
        )

    top, total = merged((local_max, local_total), ("vocab", "rows"), combine)
    logit_grads = (
        shares[:, None] * (jnp.exp(logits - top[:, None]) / total[:, None] - onehot)
    ).astype(jnp.bfloat16)
    feature_width = out_proj.shape[1]
    column_start = lax.axis_index("vocab") * feature_width
    own_terms = lax.psum_scatter(
        jnp.dot(logit_grads, head_weight, preferred_element_type=jnp.float32).astype(jnp.bfloat16),
        "rows",
        scatter_dimension=0,
        tiled=True,
    )
    grad_hidden = lax.psum(own_terms, "vocab").astype(jnp.float32)
    head_total = lax.dot_general(
        logit_grads, gathered, (((0,), (0,)), ((), ())), preferred_element_type=jnp.float32
    )
    grad_head = head_total.astype(jnp.bfloat16)
    grad_trunk = grad_hidden[:tok_local].astype(jnp.bfloat16)
    mtp_grad = grad_hidden[tok_local:]
    grad_gain = lax.psum(jnp.sum(mtp_grad * normed, axis=0), "rows")
    scaled = mtp_grad * gain
    dot_mean = jnp.mean(scaled * normed, axis=-1, keepdims=True)
    grad_residual = (inverse * (scaled - normed * dot_mean)).astype(jnp.bfloat16)
    own_columns = lax.dynamic_slice_in_dim(grad_residual, column_start, feature_width, 1)
    all_columns = lax.all_gather(own_columns, "rows", axis=0, tiled=True)
    partial_attn = lax.dot_general(
        all_columns, out_proj, (((1,), (1,)), ((), ())), preferred_element_type=jnp.float32
    )
    attn_share = lax.psum_scatter(
        partial_attn.astype(jnp.bfloat16), "vocab", scatter_dimension=0, tiled=True
    ).astype(jnp.float32)
    head_count = out_proj.shape[0] // attn_values.shape[2]
    grad_attn = attn_share.astype(jnp.bfloat16).reshape(
        attn_share.shape[0], head_count, attn_values.shape[2]
    )
    proj_grads = jnp.einsum(
        "tkh,td->khd",
        lax.all_to_all(attn_values, "rows", split_axis=1, concat_axis=0, tiled=True),
        all_columns,
        preferred_element_type=jnp.float32,
    ).astype(jnp.bfloat16)
    grad_out_proj = proj_grads.reshape(out_proj.shape[0], feature_width)
    return (grad_trunk, grad_residual, grad_gain, grad_head, grad_attn, grad_out_proj)


def solution(mesh):
    return jax.shard_map(
        local,
        mesh=mesh,
        in_specs=(
            P("rows", None),
            P("rows", None),
            P(),
            P(("vocab", "rows"), None),
            P(),
            P(),
            P("rows", None, None),
            P("rows", "vocab"),
        ),
        out_specs=(
            P("rows", None),
            P("rows", None),
            P(),
            P(("vocab", "rows"), None),
            P("vocab", "rows", None),
            P("rows", "vocab"),
        ),
        check_vma=False,
    )
```

profile of v0, /device:TPU:0, one launch (start us, length us, event | category | flops | bytes accessed | tf_op | source)
XLA Modules:
  0.0 189.2 jit_solution(16870470758866702679)
XLA Ops:
  7.2 0.0 copy-start
  7.2 0.0 reduce-scatter.3.cloned.1.call-start
  7.2 0.9 convert_element_type.38
  8.1 1.0 fusion.10
  9.1 0.9 fusion.8
  10.0 0.9 pad_maximum_fusion
  10.9 0.0 copy-start.6
  10.9 0.0 copy-start.7
  10.9 0.0 copy-start.5
  10.9 12.2 %all_gather.18 = bf16[64,7168]{1,0:T(8,128)(2,1)S(1)} all-gather(bf16[8,7168]{1,0:T(8,128)(2,1)S(1)} %pad_maximum_fusion), channel_id=1, replica_groups=mesh['vocab'=4,'rows'=8] {'rows'}, dimensions={0}, use_global_device_ids=true | all-gather | bytes 1032192 | tf_op jit(solution)/shard_map/all_gather | solution.py:58
  23.1 0.0 copy-done
  23.1 0.9 fusion.12
  24.0 0.2 exponential_reduce_fusion
  24.2 0.3 dynamic-update-slice
  24.5 0.3 dynamic-update-slice.1
  24.8 39.6 %all-reduce.2 = (f32[2048]{0:T(1024)S(1)}, f32[2048]{0:T(1024)S(1)}) all-reduce(f32[2048]{0:T(1024)S(1)} %dynamic-update-slice, f32[2048]{0:T(1024)S(1)} %dynamic-update-slice.1), channel_id=2, replica_groups=mesh['vocab'=4,'rows'=8] {'vocab','rows'}, use_global_device_ids=true, to_apply=%add | all-reduce | flops 4096 | bytes 32768
  64.3 0.1 reshape.41
  64.4 0.1 reshape.42
  64.5 1.4 while.17
  65.9 0.0 copy-done.6
  65.9 0.0 copy-start.4
  65.9 0.1 stack_reshape.7
  66.0 0.0 copy-done.7
  66.0 0.1 stack_reshape.6
  66.1 0.1 eq.15
  66.2 0.0 copy-done.5
  66.2 1.4 convolution_convert_fusion.1
  67.6 0.0 reduce-scatter.3.cloned.1.call-update
  67.6 0.0 copy-done.4
  67.7 0.6 copy.21
  68.3 4.5 %all-to-all-start = ((bf16[4,16,128]{2,0,1:T(4,128)(2,1)}), bf16[4,16,128]{2,0,1:T(4,128)(2,1)S(1)}, u32[]{:S(2)}, u32[]{:S(2)}) async-start(bf16[4,16,128]{2,0,1:T(4,128)(2,1)} %copy.21), calls=%async_computation.2 | async-start | bytes 32768 | tf_op jit(solution)/shard_map/all_to_all | solution.py:109
  72.8 0.0 all-reduce.5.cloned.1.call-start
  72.8 31.1 %reduce-scatter.3.cloned.1.call-done = bf16[8,7168]{1,0:T(8,128)(2,1)} async-done(((bf16[64,7168]{1,0:T(8,128)(2,1)}), bf16[8,7168]{1,0:T(8,128)(2,1)}) %reduce-scatter.3.cloned.1.call-update) | async-done | bytes 114704 | tf_op jit(solution)/shard_map/reduce_scatter | solution.py:78
  104.0 0.0 all-reduce.5.cloned.1.call-update
  104.0 0.0 reduce-scatter.5.cloned.1.call-start
  104.0 2.1 %convolution_convert_fusion = bf16[144,7168]{1,0:T(8,128)(2,1)} fusion(bf16[64,7168]{1,0:T(8,128)(2,1)S(1)} %all_gather.18, f32[64,144]{1,0:T(8,128)S(1)} %get-tuple-element.176, s32[144]{0:T(256)S(1)} %iota_add_fusion, f32[64]{0:T(128)S(1)} %get-tuple-element.140, f32[64]{0:T(128)S(1)} %get-tuple-element.139, f32[64]{0:T(128)S(1)} %copy-done.5, s32[64]{0:T(128)S(1)} %eq.15), kind=kOutput, calls=%fused_computation.6 | convolution fusion | flops 133217280 | bytes 3020352 | tf_op jit(solution)/shard_map/dot_general | solution.py:85
  106.2 0.0 all-to-all-done
  106.2 34.5 %all-reduce.5.cloned.1.call-done = bf16[8,7168]{1,0:T(8,128)(2,1)} async-done(((bf16[8,7168]{1,0:T(8,128)(2,1)}), bf16[8,7168]{1,0:T(8,128)(2,1)}) %all-reduce.5.cloned.1.call-update) | async-done | bytes 114704 | tf_op jit(solution)/shard_map/psum | solution.py:84
  140.6 1.3 fusion.11
  141.9 1.0 fusion.7
  142.9 0.0 copy-start.3
  143.0 9.2 %all-gather.2 = bf16[8,4,1792]{2,1,0:T(4,128)(2,1)S(1)} all-gather(bf16[1,4,1792]{2,1,0:T(4,128)(2,1)S(1)} %dynamic-slice_bitcast_fusion), channel_id=1, replica_groups=mesh['vocab'=4,'rows'=8] {'rows'}, dimensions={0}, use_global_device_ids=true | all-gather | bytes 129024 | tf_op jit(solution)/shard_map/all_gather | solution.py:96
  152.3 2.2 %convolution_convert_fusion.3 = bf16[32,256]{1,0:T(8,128)(2,1)} fusion(bf16[32,1792]{1,0:T(8,128)(2,1)S(1)} %reshape.52, bf16[256,1792]{1,0:T(8,128)(2,1)} %param.17), kind=kOutput, calls=%fused_computation.9 | convolution fusion | flops 29368320 | bytes 1048576 | tf_op jit(solution)/shard_map/dot_general | solution.py:97
  154.5 0.0 reduce-scatter.5.cloned.1.call-update
  154.5 1.4 convolution_convert_fusion.2
  155.9 0.6 slice.25
  156.5 24.9 %psum.15 = f32[7168]{0:T(1024)} all-reduce(f32[7168]{0:T(1024)S(1)} %get-tuple-element.159), channel_id=1, replica_groups=mesh['vocab'=4,'rows'=8] {'rows'}, use_global_device_ids=true, to_apply=%region_9.0 | all-reduce | flops 7168 | bytes 57344 | tf_op jit(solution)/shard_map/psum | solution.py:91
  181.4 1.3 copy.23
  (50 shorter events, 1.0 us)
Async XLA Ops:
  7.2 15.9 %copy-start = (bf16[144,7168]{1,0:T(8,128)(2,1)S(1)}, bf16[144,7168]{1,0:T(8,128)(2,1)}, u32[]{:S(2)}) copy-start(bf16[144,7168]{1,0:T(8,128)(2,1)} %param.13) | copy-start | bytes 6193156
  7.2 96.8 %reduce-scatter.3.cloned.1.call-start = ((), (), s32[]{:S(2)}) async-start(), calls=%async_computation.3 | async-start | bytes 1032192 | tf_op jit(solution)/shard_map/reduce_scatter | solution.py:78
  10.9 55.0 %copy-start.6 = (s32[32]{0:T(128)S(1)}, s32[32]{0:T(128)}, u32[]{:S(2)}) copy-start(s32[32]{0:T(128)} %param.15) | copy-start | bytes 388
  10.9 55.1 %copy-start.7 = (s32[32]{0:T(128)S(1)}, s32[32]{0:T(128)}, u32[]{:S(2)}) copy-start(s32[32]{0:T(128)} %param.14) | copy-start | bytes 388
  10.9 55.3 %copy-start.5 = (f32[64]{0:T(128)S(1)}, f32[64]{0:T(128)}, u32[]{:S(2)}) copy-start(f32[64]{0:T(128)} %constant.55.clone.1) | copy-start | bytes 772
  65.9 1.8 copy-start.4
  67.6 73.0 %copy-start.1 = (bf16[4,7168]{1,0:T(4,128)(2,1)S(1)}, bf16[4,7168]{1,0:T(4,128)(2,1)}, u32[]{:S(2)}) copy-start(bf16[4,7168]{1,0:T(4,128)(2,1)} %param.11) | copy-start | bytes 172036
  68.3 37.9 %all-to-all-start = ((bf16[4,16,128]{2,0,1:T(4,128)(2,1)}), bf16[4,16,128]{2,0,1:T(4,128)(2,1)S(1)}, u32[]{:S(2)}, u32[]{:S(2)}) async-start(bf16[4,16,128]{2,0,1:T(4,128)(2,1)} %copy.21), calls=%async_computation.2 | async-start | bytes 32768 | tf_op jit(solution)/shard_map/all_to_all | solution.py:109
  72.8 67.9 %all-reduce.5.cloned.1.call-start = ((), (), s32[]{:S(2)}) async-start(), calls=%async_computation.4 | async-start | bytes 229376 | tf_op jit(solution)/shard_map/psum | solution.py:84
  104.0 77.4 %reduce-scatter.5.cloned.1.call-start = ((), (), s32[]{:S(2)}) async-start(), calls=%async_computation.5 | async-start | bytes 20480 | tf_op jit(solution)/shard_map/reduce_scatter | solution.py:100
  140.6 15.2 %copy-start.2 = (bf16[8,7168]{1,0:T(8,128)(2,1)S(1)}, bf16[8,7168]{1,0:T(8,128)(2,1)}, u32[]{:S(2)}) copy-start(bf16[8,7168]{1,0:T(8,128)(2,1)} %all-reduce.5.cloned.1.call-done) | copy-start | bytes 344068
  142.9 39.7 %copy-start.3 = (bf16[4,7168]{1,0:T(4,128)(2,1)}, bf16[4,7168]{1,0:T(4,128)(2,1)S(1)}, u32[]{:S(2)}) copy-start(bf16[4,7168]{1,0:T(4,128)(2,1)S(1)} %fusion.7) | copy-start | bytes 172036
Sparse Core Ops, SparseCore 0:
  67.8 36.1 reduce-scatter.2
  106.3 34.3 all-reduce.4
  154.6 18.2 reduce-scatter.4
where the time goes:
time: 190 us; the launch traced here: 189 us
  blocking collectives  85.8 us (45%)
  waiting for transfers between devices  65.6 us (35%)
  between operations  13.9 us (7%)
  matrix products  8.03 us (4%)
  other arithmetic  7 us (4%)
  starting transfers between devices  4.63 us (2%)
  local copies, waits for them, and re-layouts  3.6 us (2%)
    unnamed x1, blocking collectives  39.6 us
    psum x1, waiting for transfers between devices, local(): grad_hidden = lax.psum(own_terms, 'vocab').astype(jnp.float32)  34.5 us
    reduce_scatter x1, waiting for transfers between devices, local(): lax.psum_scatter(jnp.dot(logit_grads, head_weight, preferred_element_type...  31.1 us
    psum x1, blocking collectives, local(): grad_gain = lax.psum(jnp.sum(mtp_grad * normed, axis=0), 'rows')  24.9 us
    all_gather x1, blocking collectives, local(): gathered = lax.all_gather(stacked, 'rows', axis=0, tiled=True)  12.2 us
    all_gather x1, blocking collectives, local(): all_columns = lax.all_gather(own_columns, 'rows', axis=0, tiled=True)  9.22 us
    all_to_all x1, starting transfers between devices, local(): lax.all_to_all(attn_values, 'rows', split_axis=1, concat_axis=0, tiled=True)  4.52 us
  transfers between devices with their start and end apart: 4, of which 2 were waited for; matrix products, arithmetic and copies ran while one was open for 3% of the time, Pallas kernels for 0%

commit v1 on v0

--- a/solution.py
+++ b/solution.py
@@ -88,7 +88,7 @@
     grad_head = head_total.astype(jnp.bfloat16)
     grad_trunk = grad_hidden[:tok_local].astype(jnp.bfloat16)
     mtp_grad = grad_hidden[tok_local:]
-    grad_gain = lax.psum(jnp.sum(mtp_grad * normed, axis=0), "rows")
+    grad_gain = jnp.sum(lax.all_gather(jnp.sum(mtp_grad * normed, axis=0), "rows"), axis=0)
     scaled = mtp_grad * gain
     dot_mean = jnp.mean(scaled * normed, axis=-1, keepdims=True)
     grad_residual = (inverse * (scaled - normed * dot_mean)).astype(jnp.bfloat16)

time: 190 us -> 181 us (0.953)
  blocking collectives: 85.8 us -> 70.2 us
  waiting for transfers between devices: 65.6 us -> 72.1 us
    psum x1 -> x0, blocking collectives: 24.9 us -> none  [local(): grad_gain = lax.psum(jnp.sum(mtp_grad * normed, axis=0), 'rows')]
    all_gather x0 -> x1, blocking collectives: none -> 9.23 us  [local(): lax.all_gather(jnp.sum(mtp_grad * normed, axis=0), 'rows')]
    reduce_scatter x1, waiting for transfers between devices: 0.01 us -> 6.49 us  [local(): lax.psum_scatter(partial_attn.astype(jnp.bfloat16), 'vocab', scatter_dime...]
  transfers between devices with their start and end apart: 4 -> 4, of which waited for: 2 -> 3; matrix products, arithmetic and copies ran while one was open for 3% -> 3% of each run, Pallas kernels for 0% -> 0%
where the time goes in v1:
time: 181 us
  waiting for transfers between devices  72.1 us (40%)
  blocking collectives  70.2 us (39%)
  between operations  13.9 us (8%)
  matrix products  8.03 us (4%)
  other arithmetic  7.66 us (4%)
  starting transfers between devices  4.63 us (3%)
  local copies, waits for them, and re-layouts  3.64 us (2%)
    unnamed x1, blocking collectives  39.6 us
    psum x1, waiting for transfers between devices, local(): grad_hidden = lax.psum(own_terms, 'vocab').astype(jnp.float32)  34.5 us
    reduce_scatter x1, waiting for transfers between devices, local(): lax.psum_scatter(jnp.dot(logit_grads, head_weight, preferred_element_type...  31.1 us
    all_gather x1, blocking collectives, local(): gathered = lax.all_gather(stacked, 'rows', axis=0, tiled=True)  12.2 us
    all_gather x1, blocking collectives, local(): lax.all_gather(jnp.sum(mtp_grad * normed, axis=0), 'rows')  9.23 us
    all_gather x1, blocking collectives, local(): all_columns = lax.all_gather(own_columns, 'rows', axis=0, tiled=True)  9.22 us
    reduce_scatter x1, waiting for transfers between devices, local(): lax.psum_scatter(partial_attn.astype(jnp.bfloat16), 'vocab', scatter_dime...  6.49 us
    all_to_all x1, starting transfers between devices, local(): lax.all_to_all(attn_values, 'rows', split_axis=1, concat_axis=0, tiled=True)  4.52 us
  transfers between devices with their start and end apart: 4, of which 3 were waited for; matrix products, arithmetic and copies ran while one was open for 3% of the time, Pallas kernels for 0%

profile of v1, /device:TPU:0, one launch (start us, length us, event | category | flops | bytes accessed | tf_op | source)
XLA Modules:
  0.0 180.7 jit_solution(9579891943069815210)
XLA Ops:
  7.2 0.0 copy-start
  7.2 0.0 reduce-scatter.3.cloned.1.call-start
  7.2 0.9 convert_element_type.38
  8.1 1.0 fusion.10
  9.1 0.9 fusion.8
  10.0 0.9 pad_maximum_fusion
  10.9 0.0 copy-start.6
  10.9 0.0 copy-start.7
  10.9 0.0 copy-start.5
  10.9 12.2 %all_gather.24 = bf16[64,7168]{1,0:T(8,128)(2,1)S(1)} all-gather(bf16[8,7168]{1,0:T(8,128)(2,1)S(1)} %pad_maximum_fusion), channel_id=1, replica_groups=mesh['vocab'=4,'rows'=8] {'rows'}, dimensions={0}, use_global_device_ids=true | all-gather | bytes 1032192 | tf_op jit(solution)/shard_map/all_gather | solution.py:58
  23.1 0.0 copy-done
  23.1 0.9 fusion.12
  24.0 0.2 exponential_reduce_fusion
  24.2 0.3 dynamic-update-slice
  24.5 0.3 dynamic-update-slice.1
  24.8 39.6 %all-reduce.2 = (f32[2048]{0:T(1024)S(1)}, f32[2048]{0:T(1024)S(1)}) all-reduce(f32[2048]{0:T(1024)S(1)} %dynamic-update-slice, f32[2048]{0:T(1024)S(1)} %dynamic-update-slice.1), channel_id=2, replica_groups=mesh['vocab'=4,'rows'=8] {'vocab','rows'}, use_global_device_ids=true, to_apply=%add | all-reduce | flops 4096 | bytes 32768
  64.3 0.1 reshape.41
  64.4 0.1 reshape.42
  64.5 1.4 while.17
  65.9 0.0 copy-done.6
  65.9 0.0 copy-start.4
  65.9 0.1 stack_reshape.7
  66.0 0.1 stack_reshape.6
  66.1 0.1 eq.15
  66.2 1.4 convolution_convert_fusion.1
  67.6 0.0 reduce-scatter.3.cloned.1.call-update
  67.6 0.6 copy.25
  68.3 4.5 %all-to-all-start = ((bf16[4,16,128]{2,0,1:T(4,128)(2,1)}), bf16[4,16,128]{2,0,1:T(4,128)(2,1)S(1)}, u32[]{:S(2)}, u32[]{:S(2)}) async-start(bf16[4,16,128]{2,0,1:T(4,128)(2,1)} %copy.25), calls=%async_computation.2 | async-start | bytes 32768 | tf_op jit(solution)/shard_map/all_to_all | solution.py:109
  72.8 0.0 all-reduce.5.cloned.1.call-start
  72.8 31.1 %reduce-scatter.3.cloned.1.call-done = bf16[8,7168]{1,0:T(8,128)(2,1)} async-done(((bf16[64,7168]{1,0:T(8,128)(2,1)}), bf16[8,7168]{1,0:T(8,128)(2,1)}) %reduce-scatter.3.cloned.1.call-update) | async-done | bytes 114704 | tf_op jit(solution)/shard_map/reduce_scatter | solution.py:78
  103.9 0.0 all-reduce.5.cloned.1.call-update
  104.0 0.0 reduce-scatter.5.cloned.1.call-start
  104.0 2.1 %convolution_convert_fusion = bf16[144,7168]{1,0:T(8,128)(2,1)} fusion(bf16[64,7168]{1,0:T(8,128)(2,1)S(1)} %all_gather.24, f32[64,144]{1,0:T(8,128)S(1)} %get-tuple-element.182, s32[144]{0:T(256)S(1)} %iota_add_fusion, f32[64]{0:T(128)S(1)} %get-tuple-element.140, f32[64]{0:T(128)S(1)} %get-tuple-element.139, f32[64]{0:T(128)S(1)} %copy-done.5, s32[64]{0:T(128)S(1)} %eq.15), kind=kOutput, calls=%fused_computation.6 | convolution fusion | flops 133217280 | bytes 3020352 | tf_op jit(solution)/shard_map/dot_general | solution.py:85
  106.1 0.0 all-to-all-done
  106.2 34.5 %all-reduce.5.cloned.1.call-done = bf16[8,7168]{1,0:T(8,128)(2,1)} async-done(((bf16[8,7168]{1,0:T(8,128)(2,1)}), bf16[8,7168]{1,0:T(8,128)(2,1)}) %all-reduce.5.cloned.1.call-update) | async-done | bytes 114704 | tf_op jit(solution)/shard_map/psum | solution.py:84
  140.6 1.3 fusion.11
  141.9 1.0 fusion.7
  142.9 0.0 copy-start.3
  143.0 9.2 %all-gather.3 = bf16[8,4,1792]{2,1,0:T(4,128)(2,1)S(1)} all-gather(bf16[1,4,1792]{2,1,0:T(4,128)(2,1)S(1)} %dynamic-slice_bitcast_fusion), channel_id=1, replica_groups=mesh['vocab'=4,'rows'=8] {'rows'}, dimensions={0}, use_global_device_ids=true | all-gather | bytes 129024 | tf_op jit(solution)/shard_map/all_gather | solution.py:96
  152.3 2.2 %convolution_convert_fusion.3 = bf16[32,256]{1,0:T(8,128)(2,1)} fusion(bf16[32,1792]{1,0:T(8,128)(2,1)S(1)} %reshape.53, bf16[256,1792]{1,0:T(8,128)(2,1)} %param.17), kind=kOutput, calls=%fused_computation.9 | convolution fusion | flops 29368320 | bytes 1048576 | tf_op jit(solution)/shard_map/dot_general | solution.py:97
  154.5 0.0 reduce-scatter.5.cloned.1.call-update
  154.5 1.4 convolution_convert_fusion.2
  155.9 9.2 %all-gather.2 = f32[57344]{0:T(1024)S(1)} all-gather(f32[7168]{0:T(1024)S(1)} %get-tuple-element.165), channel_id=4, replica_groups=mesh['vocab'=4,'rows'=8] {'rows'}, dimensions={0}, use_global_device_ids=true | all-gather | bytes 258048 | tf_op jit(solution)/shard_map/all_gather | solution.py:91
  165.1 0.7 reduce_sum.49
  165.8 0.6 slice.25
  166.4 6.5 %reduce-scatter.5.cloned.1.call-done = bf16[8,256]{1,0:T(8,128)(2,1)} async-done(((bf16[32,256]{1,0:T(8,128)(2,1)}), bf16[8,256]{1,0:T(8,128)(2,1)}) %reduce-scatter.5.cloned.1.call-update) | async-done | bytes 4112 | tf_op jit(solution)/shard_map/reduce_scatter | solution.py:100
  172.9 1.3 copy.27
  174.2 0.0 copy-done.3
  (52 shorter events, 1.0 us)
Async XLA Ops:
  7.2 15.9 %copy-start = (bf16[144,7168]{1,0:T(8,128)(2,1)S(1)}, bf16[144,7168]{1,0:T(8,128)(2,1)}, u32[]{:S(2)}) copy-start(bf16[144,7168]{1,0:T(8,128)(2,1)} %param.13) | copy-start | bytes 6193156
  7.2 96.8 %reduce-scatter.3.cloned.1.call-start = ((), (), s32[]{:S(2)}) async-start(), calls=%async_computation.3 | async-start | bytes 1032192 | tf_op jit(solution)/shard_map/reduce_scatter | solution.py:78
  10.9 55.0 %copy-start.6 = (s32[32]{0:T(128)S(1)}, s32[32]{0:T(128)}, u32[]{:S(2)}) copy-start(s32[32]{0:T(128)} %param.15) | copy-start | bytes 388
  10.9 55.1 %copy-start.7 = (s32[32]{0:T(128)S(1)}, s32[32]{0:T(128)}, u32[]{:S(2)}) copy-start(s32[32]{0:T(128)} %param.14) | copy-start | bytes 388
  10.9 55.3 %copy-start.5 = (f32[64]{0:T(128)S(1)}, f32[64]{0:T(128)}, u32[]{:S(2)}) copy-start(f32[64]{0:T(128)} %constant.55.clone.1) | copy-start | bytes 772
  65.9 1.8 copy-start.4
  67.6 73.0 %copy-start.1 = (bf16[4,7168]{1,0:T(4,128)(2,1)S(1)}, bf16[4,7168]{1,0:T(4,128)(2,1)}, u32[]{:S(2)}) copy-start(bf16[4,7168]{1,0:T(4,128)(2,1)} %param.11) | copy-start | bytes 172036
  68.3 37.9 %all-to-all-start = ((bf16[4,16,128]{2,0,1:T(4,128)(2,1)}), bf16[4,16,128]{2,0,1:T(4,128)(2,1)S(1)}, u32[]{:S(2)}, u32[]{:S(2)}) async-start(bf16[4,16,128]{2,0,1:T(4,128)(2,1)} %copy.25), calls=%async_computation.2 | async-start | bytes 32768 | tf_op jit(solution)/shard_map/all_to_all | solution.py:109
  72.8 67.9 %all-reduce.5.cloned.1.call-start = ((), (), s32[]{:S(2)}) async-start(), calls=%async_computation.4 | async-start | bytes 229376 | tf_op jit(solution)/shard_map/psum | solution.py:84
  104.0 69.0 %reduce-scatter.5.cloned.1.call-start = ((), (), s32[]{:S(2)}) async-start(), calls=%async_computation.5 | async-start | bytes 20480 | tf_op jit(solution)/shard_map/reduce_scatter | solution.py:100
  140.6 25.2 %copy-start.2 = (bf16[8,7168]{1,0:T(8,128)(2,1)S(1)}, bf16[8,7168]{1,0:T(8,128)(2,1)}, u32[]{:S(2)}) copy-start(bf16[8,7168]{1,0:T(8,128)(2,1)} %all-reduce.5.cloned.1.call-done) | copy-start | bytes 344068
  142.9 31.3 %copy-start.3 = (bf16[4,7168]{1,0:T(4,128)(2,1)}, bf16[4,7168]{1,0:T(4,128)(2,1)S(1)}, u32[]{:S(2)}) copy-start(bf16[4,7168]{1,0:T(4,128)(2,1)S(1)} %fusion.7) | copy-start | bytes 172036
Sparse Core Ops, SparseCore 0:
  67.8 36.1 reduce-scatter.2
  106.3 34.3 all-reduce.4
  154.6 18.2 reduce-scatter.4
